TPU v7x, 128 devices: a whole 4x4x4 slice. The times are simulated.
128 devices in a mesh: row: 64 (over z, y, x), pan: 2 (over core).
Axes of the slice: x: 4, y: 4, z: 4, core: 2. Of those that a mesh axis runs over, the one named last changes fastest.
Arguments:
- right_side: float32 [256, 65536], P(None, 'row'), may hold values from -6 to 6
- initial_guess: float32 [256, 65536], P(None, ('row', 'pan')), may hold values from -6 to 6
- v_factor: float32 [128, 128, 16, 512], P('row', None, 'pan'), may hold values from -0.25 to 0.25
- u_factor: float32 [128, 128, 16, 512], P('row', None, 'pan'), may hold values from -0.125 to 0.125
- tile_ranks: int32 [128, 128], P(None, 'row'), may hold values from 0 to 16
- diag_block: float32 [65536, 512], P(('row', 'pan'))
- diag_inverse: float32 [65536, 512], P(('row', 'pan'))
Outputs:
- solution: float32 [256, 65536], P(None, ('row', 'pan'))
- residual: float32 [256, 65536], P(None, ('row', 'pan'))
Inputs may be any that keep to these rules, and one draw needn't show every extreme that they name: `tile_ranks`: columns of a tile's factors from its rank on are ignored, as is the low-rank part of tile (i, i).
All inputs are finite; a program needn't handle non-finite values.
Results may differ from a plain program's by a relative error of at most 0.00017.
Values sent between devices are 32-bit elements; how exact they have to be, the bound alone decides.
A program may use at most 64 MiB of HBM per device.

v0:
```python
import jax
import jax.numpy as jnp
from jax import lax
from jax.sharding import PartitionSpec as P

ITERS = 2


def on_device(right_side, initial_guess, v_factor, u_factor, tile_ranks, diag_block, diag_inverse):
    highest = lax.Precision.HIGHEST
    pan_index = lax.axis_index("pan")
    row_index = lax.axis_index("row")
    tile_rows = v_factor.shape[0]
    tile_count = v_factor.shape[1]
    part_rank = v_factor.shape[2]
    tile_width = v_factor.shape[3]
    rhs_count = right_side.shape[0]
    own_rows = diag_block.shape[0]
    row_start = pan_index * own_rows
    tile_slot = row_start // tile_width
    components = pan_index * part_rank + jnp.arange(part_rank, dtype=jnp.int32)
    own_columns = row_index * tile_rows + jnp.arange(tile_rows, dtype=jnp.int32)
    tile_index = jnp.arange(tile_count, dtype=jnp.int32)
    off_diagonal = tile_index[:, None] != own_columns[None, :]
    rank_mask = (
        (components[None, None, :] < tile_ranks[:, :, None]) & off_diagonal[:, :, None]
    ).astype(jnp.float32)
    iterate_rows = initial_guess
    residual = initial_guess
    for iteration in range(ITERS):
        guess_full = lax.all_gather(iterate_rows, "pan", axis=1, tiled=True)
        guess_tiles = guess_full.reshape(rhs_count, tile_rows, tile_width)
        projected = jnp.einsum("cikb,rcb->ickr", v_factor, guess_tiles, precision=highest)
        projected = projected * rank_mask[:, :, :, None]
        received = lax.all_to_all(projected, "row", split_axis=0, concat_axis=1, tiled=True)
        low_rank = jnp.einsum("ickm,ickr->rim", u_factor, received, precision=highest)
        low_rank = low_rank.reshape(rhs_count, tile_rows * tile_width)
        guess_tile = lax.dynamic_slice_in_dim(guess_full, tile_slot * tile_width, tile_width, 1)
        dense_part = jnp.einsum("rb,mb->rm", guess_tile, diag_block, precision=highest)
        low_rows = lax.psum_scatter(low_rank, "pan", scatter_dimension=1, tiled=True)
        rhs_rows = lax.dynamic_slice_in_dim(right_side, row_start, own_rows, 1)
        residual = rhs_rows - (dense_part + low_rows)
        residual_full = lax.all_gather(residual, "pan", axis=1, tiled=True)
        residual_tile = lax.dynamic_slice_in_dim(
            residual_full, tile_slot * tile_width, tile_width, 1
        )
        update = jnp.einsum("rb,mb->rm", residual_tile, diag_inverse, precision=highest)
        iterate_rows = iterate_rows + update
    return (iterate_rows, residual)


def solution(mesh):
    placed = (
        P(None, "row"),
        P(None, ("row", "pan")),
        P("row", None, "pan", None),
        P("row", None, "pan", None),
        P(None, "row"),
        P(("row", "pan"), None),
        P(("row", "pan"), None),
    )
    return jax.shard_map(
        on_device,
        mesh=mesh,
        in_specs=placed,
        out_specs=(P(None, ("row", "pan")), P(None, ("row", "pan"))),
        check_vma=False,
    )
```

profile of v0, /device:TPU:1, one launch (start us, length us, event | category | flops | bytes accessed | tf_op | source)
XLA Modules:
  0.0 225.6 jit_solution(9807114171824869542)
XLA Ops:
  7.2 0.0 copy-start
  7.2 0.0 all-gather.5.cloned.1.call-start
  7.2 2.1 copy.33
  9.3 0.0 all-gather.5.cloned.1.call-update
  9.4 0.0 reduce-scatter.3.cloned.1.call-start
  9.4 0.1 iota_compare_fusion
  9.5 0.8 and_convert_fusion
  10.3 15.4 %all-gather.5.cloned.1.call-done = f32[256,1024]{0,1:T(8,128)} async-done(((f32[256,512]{0,1:T(8,128)}), f32[256,1024]{0,1:T(8,128)}) %all-gather.5.cloned.1.call-update) | async-done | bytes 1048592 | tf_op jit(solution)/shard_map/all_gather | solution.py:31
  25.7 12.3 %bitcast_multiply_fusion.1 = f32[128,2,8,256]{0,3,2,1:T(8,128)} fusion(f32[256,2,512,1]{0,2,3,1:T(8,128)} %bitcast.45, f32[2,128,8,512]{3,2,1,0:T(8,128)} %param.9, f32[128,2,8]{0,2,1:T(8,128)S(1)} %and_convert_fusion), kind=kOutput, calls=%fused_computation.5 | convolution fusion | flops 3221749760 | bytes 7348224 | tf_op jit(solution)/shard_map/cikb,rcb->ickr/dot_general | solution.py:33
  38.0 2.2 copy.36
  40.2 39.2 %all_to_all.36 = f32[128,2,8,256]{3,2,1,0:T(8,128)S(1)} all-to-all(f32[128,2,8,256]{3,2,1,0:T(8,128)S(1)} %copy.36), channel_id=1, replica_groups=mesh['row'=64,'pan'=2] {'row'}, dimensions={0} | all-to-all | bytes 4194304 | tf_op jit(solution)/shard_map/all_to_all | solution.py:35
  79.5 0.2 copy.37
  79.7 2.0 copy-done.5
  81.7 3.8 %convolution_bitcast_fusion.1 = f32[256,2,512]{2,0,1:T(8,128)S(1)} fusion(f32[2,128,8,256]{3,2,1,0:T(8,128)S(1)} %bitcast.46, f32[2,128,8,512]{3,2,1,0:T(8,128)S(1)} %copy-done.5), kind=kOutput, calls=%fused_computation.7 | convolution fusion | flops 3221225472 | bytes 7340032 | tf_op jit(solution)/shard_map/ickm,ickr->rim/dot_general | solution.py:36
  85.5 0.3 copy.38
  85.9 0.0 copy-start.4
  85.9 1.3 copy.39
  87.2 0.0 reduce-scatter.3.cloned.1.call-update
  87.2 0.0 copy-start.2
  87.2 0.0 all-gather.7.cloned.1.call-start
  87.3 9.3 %reduce-scatter.3.cloned.1.call-done = f32[256,512]{1,0:T(8,128)} async-done(((f32[256,1024]{1,0:T(8,128)}), f32[256,512]{1,0:T(8,128)}) %reduce-scatter.3.cloned.1.call-update) | async-done | bytes 524304 | tf_op jit(solution)/shard_map/reduce_scatter | solution.py:40
  96.6 0.0 copy-done
  96.6 3.9 %fusion.8 = f32[256,512]{1,0:T(8,128)} fusion(f32[256,512]{1,0:T(8,128)} %reduce-scatter.3.cloned.1.call-done, f32[512,512]{1,0:T(8,128)S(1)} %copy-done, f32[256,1024]{0,1:T(8,128)S(1)} %copy-done.4, s32[]{:T(128)S(6)} %select_n.17, f32[256,1024]{1,0:T(8,128)} %param.7, s32[]{:T(128)S(6)} %select_n.15), kind=kOutput, calls=%fused_computation.12 | convolution fusion | flops 805568512 | bytes 3145736 | tf_op jit(solution)/shard_map/rb,mb->rm/dot_general | solution.py:39
  100.5 0.0 all-gather.7.cloned.1.call-update
  100.5 0.0 all-gather.9.cloned.1.call-start
  100.6 13.2 %all-gather.7.cloned.1.call-done = f32[256,1024]{1,0:T(8,128)} async-done(((f32[256,512]{1,0:T(8,128)}), f32[256,1024]{1,0:T(8,128)}) %all-gather.7.cloned.1.call-update) | async-done | bytes 1048592 | tf_op jit(solution)/shard_map/all_gather | solution.py:43
  113.7 0.0 copy-done.2
  113.7 3.1 %convolution_add_fusion.2 = f32[256,512]{1,0:T(8,128)} fusion(f32[256,512]{1,0:T(8,128)} %param.8, f32[512,512]{1,0:T(8,128)S(1)} %copy-done.2, f32[256,1024]{1,0:T(8,128)} %all-gather.7.cloned.1.call-done, s32[]{:T(128)S(6)} %select_n.17), kind=kOutput, calls=%fused_computation.10 | convolution fusion | flops 805437440 | bytes 2621444 | tf_op jit(solution)/shard_map/rb,mb->rm/dot_general | solution.py:47
  116.8 0.0 all-gather.9.cloned.1.call-update
  116.8 0.3 reduce-scatter.5.cloned.1.call-start
  117.1 13.0 %all-gather.9.cloned.1.call-done = f32[256,1024]{1,0:T(8,128)} async-done(((f32[256,512]{1,0:T(8,128)}), f32[256,1024]{1,0:T(8,128)}) %all-gather.9.cloned.1.call-update) | async-done | bytes 1048592 | tf_op jit(solution)/shard_map/all_gather | solution.py:31
  130.0 2.1 reshape.49
  132.1 9.3 %bitcast_multiply_fusion = f32[128,2,8,256]{0,3,2,1:T(8,128)} fusion(f32[2,128,8,512]{3,2,1,0:T(8,128)} %param.9, f32[256,2,512,1]{2,1,0,3:T(2,128)S(1)} %bitcast.44, f32[128,2,8]{0,2,1:T(8,128)S(1)} %and_convert_fusion), kind=kOutput, calls=%fused_computation.4 | convolution fusion | flops 3221749760 | bytes 7348224 | tf_op jit(solution)/shard_map/cikb,rcb->ickr/dot_general | solution.py:33
  141.4 2.2 copy.42
  143.7 39.2 %all_to_all.37 = f32[128,2,8,256]{3,2,1,0:T(8,128)S(1)} all-to-all(f32[128,2,8,256]{3,2,1,0:T(8,128)S(1)} %copy.42), channel_id=1, replica_groups=mesh['row'=64,'pan'=2] {'row'}, dimensions={0} | all-to-all | bytes 4194304 | tf_op jit(solution)/shard_map/all_to_all | solution.py:35
  182.9 0.2 copy.43
  183.1 2.0 copy-done.6
  185.1 3.8 %convolution_bitcast_fusion = f32[2,32,8,512]{3,2,1,0:T(8,128)S(1)} fusion(f32[2,128,8,256]{3,2,1,0:T(8,128)S(1)} %bitcast.47, f32[2,128,8,512]{3,2,1,0:T(8,128)S(1)} %copy-done.6), kind=kOutput, calls=%fused_computation.6 | convolution fusion | flops 3221225472 | bytes 7340032 | tf_op jit(solution)/shard_map/ickm,ickr->rim/dot_general | solution.py:36
  188.9 1.1 copy.53
  190.0 0.0 reduce-scatter.5.cloned.1.call-update
  190.0 0.0 copy-start.1
  190.1 0.0 copy-start.3
  190.1 0.0 all-gather.11.cloned.1.call-start
  190.1 9.3 %reduce-scatter.5.cloned.1.call-done = f32[256,512]{1,0:T(8,128)} async-done(((f32[256,1024]{1,0:T(8,128)}), f32[256,512]{1,0:T(8,128)}) %reduce-scatter.5.cloned.1.call-update) | async-done | bytes 524304 | tf_op jit(solution)/shard_map/reduce_scatter | solution.py:40
  199.5 3.2 %fusion.9 = f32[256,512]{1,0:T(8,128)} fusion(f32[256,512]{1,0:T(8,128)} %reduce-scatter.5.cloned.1.call-done, f32[512,512]{1,0:T(8,128)S(1)} %copy-done, f32[256,1024]{1,0:T(8,128)} %all-gather.9.cloned.1.call-done, s32[]{:T(128)S(6)} %select_n.17, f32[256,1024]{1,0:T(8,128)} %param.7, s32[]{:T(128)S(6)} %select_n.15), kind=kOutput, calls=%fused_computation.13 | convolution fusion | flops 805568512 | bytes 3145736 | tf_op jit(solution)/shard_map/rb,mb->rm/dot_general | solution.py:39
  202.7 0.0 all-gather.11.cloned.1.call-update
  202.7 13.2 %all-gather.11.cloned.1.call-done = f32[256,1024]{1,0:T(8,128)} async-done(((f32[256,512]{1,0:T(8,128)}), f32[256,1024]{1,0:T(8,128)}) %all-gather.11.cloned.1.call-update) | async-done | bytes 1048592 | tf_op jit(solution)/shard_map/all_gather | solution.py:43
  215.9 2.9 %convolution_add_fusion = f32[256,512]{1,0:T(8,128)} fusion(f32[256,512]{1,0:T(8,128)S(1)} %copy-done.1, f32[512,512]{1,0:T(8,128)S(1)} %copy-done.3, f32[256,1024]{1,0:T(8,128)} %all-gather.11.cloned.1.call-done, s32[]{:T(128)S(6)} %select_n.17), kind=kOutput, calls=%fused_computation.8 | convolution fusion | flops 805437440 | bytes 2621444 | tf_op jit(solution)/shard_map/rb,mb->rm/dot_general | solution.py:47
  (7 shorter events, 0.0 us)
Async XLA Ops:
  7.2 89.5 %copy-start = (f32[512,512]{1,0:T(8,128)S(1)}, f32[512,512]{1,0:T(8,128)}, u32[]{:S(2)}) copy-start(f32[512,512]{1,0:T(8,128)} %param.12) | copy-start | bytes 3145732
  7.2 18.5 %all-gather.5.cloned.1.call-start = ((), (), s32[]{:S(2)}) async-start(), calls=%async_computation.4 | async-start | bytes 1572864 | tf_op jit(solution)/shard_map/all_gather | solution.py:31
  9.4 87.3 %reduce-scatter.3.cloned.1.call-start = ((), (), s32[]{:S(2)}) async-start(), calls=%async_computation.5 | async-start | bytes 1572864 | tf_op jit(solution)/shard_map/reduce_scatter | solution.py:40
  79.5 2.2 copy-start.5
  85.9 10.8 %copy-start.4 = (f32[256,1024]{0,1:T(8,128)S(1)}, f32[256,1024]{0,1:T(8,128)}, u32[]{:S(2)}) copy-start(f32[256,1024]{0,1:T(8,128)} %all-gather.5.cloned.1.call-done) | copy-start | bytes 3145732
  87.2 26.5 %copy-start.2 = (f32[512,512]{1,0:T(8,128)S(1)}, f32[512,512]{1,0:T(8,128)}, u32[]{:S(2)}) copy-start(f32[512,512]{1,0:T(8,128)} %param.13) | copy-start | bytes 3145732
  87.2 26.5 %all-gather.7.cloned.1.call-start = ((), (), s32[]{:S(2)}) async-start(), calls=%async_computation.6 | async-start | bytes 1572864 | tf_op jit(solution)/shard_map/all_gather | solution.py:43
  100.5 29.5 %all-gather.9.cloned.1.call-start = ((), (), s32[]{:S(2)}) async-start(), calls=%async_computation.7 | async-start | bytes 1572864 | tf_op jit(solution)/shard_map/all_gather | solution.py:31
  116.8 82.6 %reduce-scatter.5.cloned.1.call-start = ((), (), s32[]{:S(2)}) async-start(), calls=%async_computation.8 | async-start | bytes 1572864 | tf_op jit(solution)/shard_map/reduce_scatter | solution.py:40
  182.9 2.2 copy-start.6
  190.0 25.9 %copy-start.1 = (f32[256,512]{1,0:T(8,128)S(1)}, f32[256,512]{1,0:T(8,128)}, u32[]{:S(2)}) copy-start(f32[256,512]{1,0:T(8,128)} %convolution_add_fusion.2) | copy-start | bytes 1572868
  190.1 25.9 %copy-start.3 = (f32[512,512]{1,0:T(8,128)S(1)}, f32[512,512]{1,0:T(8,128)}, u32[]{:S(2)}) copy-start(f32[512,512]{1,0:T(8,128)} %param.13) | copy-start | bytes 3145732
  190.1 25.8 %all-gather.11.cloned.1.call-start = ((), (), s32[]{:S(2)}) async-start(), calls=%async_computation.9 | async-start | bytes 1572864 | tf_op jit(solution)/shard_map/all_gather | solution.py:43
Sparse Core Ops, SparseCore 0:
  10.2 15.3 all-gather.4
  87.3 9.2 reduce-scatter.2
  100.6 13.0 all-gather.6
  116.9 13.0 all-gather.8
  190.2 9.2 reduce-scatter.4
  202.8 13.0 all-gather.10
where the time goes:
time: 226 us
  blocking collectives  78.5 us (35%)
  waiting for transfers between devices  73.5 us (33%)
  matrix products  42.3 us (19%)
  local copies, waits for them, and re-layouts  15.8 us (7%)
  between operations  14.3 us (6%)
    all_to_all x2, blocking collectives, on_device(): lax.all_to_all(projected, 'row', split_axis=0, concat_axis=1, tiled=True)  78.5 us
    all_gather x2, waiting for transfers between devices, on_device(): guess_full = lax.all_gather(iterate_rows, 'pan', axis=1, tiled=True)  28.3 us
    all_gather x2, waiting for transfers between devices, on_device(): residual_full = lax.all_gather(residual, 'pan', axis=1, tiled=True)  26.4 us
    dot_general x2, matrix products, on_device(): jnp.einsum('cikb,rcb->ickr', v_factor, guess_tiles, precision=highest)  21.6 us
    reduce_scatter x2, waiting for transfers between devices, on_device(): lax.psum_scatter(low_rank, 'pan', scatter_dimension=1, tiled=True)  18.7 us
    dot_general x2, matrix products, on_device(): jnp.einsum('ickm,ickr->rim', u_factor, received, precision=highest)  7.64 us
    dot_general x2, matrix products, on_device(): jnp.einsum('rb,mb->rm', guess_tile, diag_block, precision=highest)  7.07 us
    unnamed x15, local copies, waits for them, and re-layouts  6.15 us
  transfers between devices with their start and end apart: 6, of which 6 were waited for; matrix products, arithmetic and copies ran while one was open for 0% of the time, Pallas kernels for 0%

commit v1 on v0

--- a/solution.py
+++ b/solution.py
@@ -40,7 +40,12 @@
         low_rows = lax.psum_scatter(low_rank, "pan", scatter_dimension=1, tiled=True)
         rhs_rows = lax.dynamic_slice_in_dim(right_side, row_start, own_rows, 1)
         residual = rhs_rows - (dense_part + low_rows)
-        residual_full = lax.all_gather(residual, "pan", axis=1, tiled=True)
+        residual_full = jnp.concatenate(
+            jax.lax.all_to_all(
+                jnp.stack([residual for _ in range(jax.lax.axis_size("pan"))], axis=0), "pan", 0, 0
+            ),
+            axis=1,
+        )
         residual_tile = lax.dynamic_slice_in_dim(
             residual_full, tile_slot * tile_width, tile_width, 1
         )

time: 226 us -> 213 us (0.942)
  waiting for transfers between devices: 73.5 us -> 47.4 us
  blocking collectives: 78.5 us -> 88.1 us
  local copies, waits for them, and re-layouts: 15.8 us -> 19.1 us
    all_gather x2 -> x0, waiting for transfers between devices: 26.4 us -> none  [on_device(): residual_full = lax.all_gather(residual, 'pan', axis=1, tiled=True)]
    all_to_all x0 -> x2, blocking collectives: none -> 9.65 us  [on_device(): jax.lax.all_to_all(jnp.stack([residual for _ in range(jax.lax.axis_size('...]
    reshape x0 -> x2, local copies, waits for them, and re-layouts: none -> 3.86 us  [on_device(): jnp.concatenate(jax.lax.all_to_all(jnp.stack([residual for _ in range(jax...]
    unnamed x15 -> x21, local copies, waits for them, and re-layouts: 6.15 us -> 6.17 us
  transfers between devices with their start and end apart: 6 -> 4, of which waited for: 6 -> 4; matrix products, arithmetic and copies ran while one was open for 0% -> 0% of each run, Pallas kernels for 0% -> 0%
where the time goes in v1:
time: 213 us; the launch traced here: 212 us
  blocking collectives  88.1 us (41%)
  waiting for transfers between devices  47.4 us (22%)
  matrix products  42 us (20%)
  local copies, waits for them, and re-layouts  19.1 us (9%)
  between operations  14 us (7%)
    all_to_all x2, blocking collectives, on_device(): lax.all_to_all(projected, 'row', split_axis=0, concat_axis=1, tiled=True)  78.5 us
    all_gather x2, waiting for transfers between devices, on_device(): guess_full = lax.all_gather(iterate_rows, 'pan', axis=1, tiled=True)  28.6 us
    dot_general x2, matrix products, on_device(): jnp.einsum('cikb,rcb->ickr', v_factor, guess_tiles, precision=highest)  21.6 us
    reduce_scatter x2, waiting for transfers between devices, on_device(): lax.psum_scatter(low_rank, 'pan', scatter_dimension=1, tiled=True)  18.8 us
    all_to_all x2, blocking collectives, on_device(): jax.lax.all_to_all(jnp.stack([residual for _ in range(jax.lax.axis_size('...  9.65 us
    dot_general x2, matrix products, on_device(): jnp.einsum('ickm,ickr->rim', u_factor, received, precision=highest)  7.65 us
    dot_general x2, matrix products, on_device(): jnp.einsum('rb,mb->rm', residual_tile, diag_inverse, precision=highest)  7.57 us
    unnamed x21, local copies, waits for them, and re-layouts  6.17 us
  transfers between devices with their start and end apart: 4, of which 4 were waited for; matrix products, arithmetic and copies ran while one was open for 0% of the time, Pallas kernels for 0%

profile of v1, /device:TPU:1, one launch (start us, length us, event | category | flops | bytes accessed | tf_op | source)
XLA Modules:
  0.0 212.1 jit_solution(2231467667311967014)
XLA Ops:
  7.2 0.0 copy-start
  7.2 0.0 all-gather.3.cloned.1.call-start
  7.2 2.1 copy.35
  9.3 0.0 all-gather.3.cloned.1.call-update
  9.4 0.0 reduce-scatter.3.cloned.1.call-start
  9.4 0.1 iota_compare_fusion
  9.5 0.8 and_convert_fusion
  10.3 15.4 %all-gather.3.cloned.1.call-done = f32[256,1024]{0,1:T(8,128)} async-done(((f32[256,512]{0,1:T(8,128)}), f32[256,1024]{0,1:T(8,128)}) %all-gather.3.cloned.1.call-update) | async-done | bytes 1048592 | tf_op jit(solution)/shard_map/all_gather | solution.py:31
  25.7 12.3 %bitcast_multiply_fusion.1 = f32[128,2,8,256]{0,3,2,1:T(8,128)} fusion(f32[256,2,512,1]{0,2,3,1:T(8,128)} %bitcast.57, f32[2,128,8,512]{3,2,1,0:T(8,128)} %param.9, f32[128,2,8]{0,2,1:T(8,128)S(1)} %and_convert_fusion), kind=kOutput, calls=%fused_computation.5 | convolution fusion | flops 3221749760 | bytes 7348224 | tf_op jit(solution)/shard_map/cikb,rcb->ickr/dot_general | solution.py:33
  38.0 2.2 %copy.38 = f32[128,2,8,256]{3,2,1,0:T(8,128)S(1)} copy(f32[128,2,8,256]{0,3,2,1:T(8,128)} %bitcast_multiply_fusion.1) | data formatting | bytes 4194304 | tf_op jit(solution)/shard_map/mul | solution.py:34
  40.2 39.2 %all_to_all.46 = f32[128,2,8,256]{3,2,1,0:T(8,128)S(1)} all-to-all(f32[128,2,8,256]{3,2,1,0:T(8,128)S(1)} %copy.38), channel_id=1, replica_groups=mesh['row'=64,'pan'=2] {'row'}, dimensions={0} | all-to-all | bytes 4194304 | tf_op jit(solution)/shard_map/all_to_all | solution.py:35
  79.5 0.2 copy.39
  79.7 2.0 copy-done.8
  81.7 3.8 %convolution_bitcast_fusion.1 = f32[2,32,8,512]{3,2,1,0:T(8,128)S(1)} fusion(f32[2,128,8,256]{3,2,1,0:T(8,128)S(1)} %bitcast.58, f32[2,128,8,512]{3,2,1,0:T(8,128)S(1)} %copy-done.8), kind=kOutput, calls=%fused_computation.7 | convolution fusion | flops 3221225472 | bytes 7340032 | tf_op jit(solution)/shard_map/ickm,ickr->rim/dot_general | solution.py:36
  85.5 0.0 copy-start.5
  85.5 0.0 copy-start.7
  85.5 1.1 copy.56
  86.6 0.0 reduce-scatter.3.cloned.1.call-update
  86.6 0.0 all-gather.5.cloned.1.call-start
  86.7 9.3 %reduce-scatter.3.cloned.1.call-done = f32[256,512]{1,0:T(8,128)} async-done(((f32[256,1024]{1,0:T(8,128)}), f32[256,512]{1,0:T(8,128)}) %reduce-scatter.3.cloned.1.call-update) | async-done | bytes 524304 | tf_op jit(solution)/shard_map/reduce_scatter | solution.py:40
  96.0 2.9 %fusion.9 = f32[1,256,512]{2,1,0:T(8,128)S(1)} fusion(f32[256,512]{1,0:T(8,128)} %reduce-scatter.3.cloned.1.call-done, f32[512,512]{1,0:T(8,128)S(1)} %copy-done, f32[256,1024]{0,1:T(8,128)S(1)} %copy-done.5, s32[]{:T(128)S(6)} %select_n.17, f32[256,1024]{1,0:T(8,128)S(1)} %copy-done.7, s32[]{:T(128)S(6)} %select_n.15), kind=kOutput, calls=%fused_computation.13 | convolution fusion | flops 805568512 | bytes 3145736 | tf_op jit(solution)/shard_map/rb,mb->rm/dot_general | solution.py:39
  99.0 0.1 pad_maximum_fusion
  99.1 0.0 copy-start.2
  99.1 4.4 %all_to_all.47 = f32[2,256,512]{2,1,0:T(8,128)S(1)} all-to-all(f32[2,256,512]{2,1,0:T(8,128)S(1)} %pad_maximum_fusion), channel_id=1, replica_groups=mesh['row'=64,'pan'=2] {'pan'}, dimensions={0} | all-to-all | bytes 2097152 | tf_op jit(solution)/shard_map/all_to_all | solution.py:44
  103.5 1.3 copy.41
  104.8 3.9 %convolution_add_fusion.2 = f32[256,512]{1,0:T(8,128)} fusion(f32[256,512]{1,0:T(8,128)} %param.8, f32[512,512]{1,0:T(8,128)S(1)} %copy-done.2, f32[256,1024]{0,1:T(8,128)} %bitcast.56, s32[]{:T(128)S(6)} %select_n.17), kind=kOutput, calls=%fused_computation.10 | convolution fusion | flops 805437440 | bytes 2621444 | tf_op jit(solution)/shard_map/rb,mb->rm/dot_general | solution.py:52
  108.7 0.0 all-gather.5.cloned.1.call-update
  108.7 0.3 reduce-scatter.5.cloned.1.call-start
  109.0 13.2 %all-gather.5.cloned.1.call-done = f32[256,1024]{1,0:T(8,128)} async-done(((f32[256,512]{1,0:T(8,128)}), f32[256,1024]{1,0:T(8,128)}) %all-gather.5.cloned.1.call-update) | async-done | bytes 1048592 | tf_op jit(solution)/shard_map/all_gather | solution.py:31
  122.2 2.1 reshape.63
  124.3 9.3 %bitcast_multiply_fusion = f32[128,2,8,256]{0,3,2,1:T(8,128)} fusion(f32[2,128,8,512]{3,2,1,0:T(8,128)} %param.9, f32[256,2,512,1]{2,1,0,3:T(2,128)S(1)} %bitcast.54, f32[128,2,8]{0,2,1:T(8,128)S(1)} %and_convert_fusion), kind=kOutput, calls=%fused_computation.4 | convolution fusion | flops 3221749760 | bytes 7348224 | tf_op jit(solution)/shard_map/cikb,rcb->ickr/dot_general | solution.py:33
  133.6 2.2 %copy.44 = f32[128,2,8,256]{3,2,1,0:T(8,128)S(1)} copy(f32[128,2,8,256]{0,3,2,1:T(8,128)} %bitcast_multiply_fusion) | data formatting | bytes 4194304 | tf_op jit(solution)/shard_map/mul | solution.py:34
  135.9 39.3 %all_to_all.48 = f32[128,2,8,256]{3,2,1,0:T(8,128)S(1)} all-to-all(f32[128,2,8,256]{3,2,1,0:T(8,128)S(1)} %copy.44), channel_id=1, replica_groups=mesh['row'=64,'pan'=2] {'row'}, dimensions={0} | all-to-all | bytes 4194304 | tf_op jit(solution)/shard_map/all_to_all | solution.py:35
  175.1 0.2 copy.45
  175.3 2.0 copy-done.9
  177.3 3.8 %convolution_bitcast_fusion = f32[2,32,8,512]{3,2,1,0:T(8,128)S(1)} fusion(f32[2,128,8,256]{3,2,1,0:T(8,128)S(1)} %bitcast.59, f32[2,128,8,512]{3,2,1,0:T(8,128)S(1)} %copy-done.9), kind=kOutput, calls=%fused_computation.6 | convolution fusion | flops 3221225472 | bytes 7340032 | tf_op jit(solution)/shard_map/ickm,ickr->rim/dot_general | solution.py:36
  181.2 1.1 copy.57
  182.2 0.0 reduce-scatter.5.cloned.1.call-update
  182.3 9.4 %reduce-scatter.5.cloned.1.call-done = f32[256,512]{1,0:T(8,128)} async-done(((f32[256,1024]{1,0:T(8,128)}), f32[256,512]{1,0:T(8,128)}) %reduce-scatter.5.cloned.1.call-update) | async-done | bytes 524304 | tf_op jit(solution)/shard_map/reduce_scatter | solution.py:40
  191.7 0.0 copy-done.4
  191.7 2.3 %fusion.10 = f32[256,512]{1,0:T(8,128)S(1)} fusion(f32[256,512]{1,0:T(8,128)} %reduce-scatter.5.cloned.1.call-done, f32[512,512]{1,0:T(8,128)S(1)} %copy-done, f32[256,1024]{1,0:T(8,128)S(1)} %copy-done.4, s32[]{:T(128)S(6)} %select_n.17, f32[256,1024]{1,0:T(8,128)} %param.7, s32[]{:T(128)S(6)} %select_n.15), kind=kOutput, calls=%fused_computation.14 | convolution fusion | flops 805568512 | bytes 3145736 | tf_op jit(solution)/shard_map/rb,mb->rm/dot_general | solution.py:39
  193.9 0.0 copy-start.6
  193.9 0.1 pad_maximum_fusion.1
  194.1 0.0 copy-start.1
  194.1 0.0 copy-start.3
  194.1 5.2 %all_to_all.49 = f32[2,256,512]{2,1,0:T(8,128)} all-to-all(f32[2,256,512]{2,1,0:T(8,128)S(1)} %pad_maximum_fusion.1), channel_id=1, replica_groups=mesh['row'=64,'pan'=2] {'pan'}, dimensions={0} | all-to-all | bytes 2097152 | tf_op jit(solution)/shard_map/all_to_all | solution.py:44
  199.3 2.5 %copy.47 = f32[256,2,512]{0,2,1:T(8,128)} copy(f32[256,2,512]{2,0,1:T(8,128)} %bitcast.53) | data formatting | bytes 2097152 | tf_op jit(solution)/shard_map/reshape | solution.py:43
  201.9 3.7 %convolution_add_fusion = f32[256,512]{1,0:T(8,128)} fusion(f32[256,512]{1,0:T(8,128)S(1)} %copy-done.1, f32[512,512]{1,0:T(8,128)S(1)} %copy-done.3, f32[256,1024]{0,1:T(8,128)} %bitcast.55, s32[]{:T(128)S(6)} %select_n.17), kind=kOutput, calls=%fused_computation.8 | convolution fusion | flops 805437440 | bytes 2621444 | tf_op jit(solution)/shard_map/rb,mb->rm/dot_general | solution.py:52
  (12 shorter events, 0.0 us)
Async XLA Ops:
  7.2 88.9 %copy-start = (f32[512,512]{1,0:T(8,128)S(1)}, f32[512,512]{1,0:T(8,128)}, u32[]{:S(2)}) copy-start(f32[512,512]{1,0:T(8,128)} %param.12) | copy-start | bytes 3145732
  7.2 18.5 %all-gather.3.cloned.1.call-start = ((), (), s32[]{:S(2)}) async-start(), calls=%async_computation.6 | async-start | bytes 1572864 | tf_op jit(solution)/shard_map/all_gather | solution.py:31
  9.4 86.7 %reduce-scatter.3.cloned.1.call-start = ((), (), s32[]{:S(2)}) async-start(), calls=%async_computation.7 | async-start | bytes 1572864 | tf_op jit(solution)/shard_map/reduce_scatter | solution.py:40
  79.5 2.2 %copy-start.8 = (f32[2,128,8,512]{3,2,1,0:T(8,128)S(1)}, f32[2,128,8,512]{3,2,1,0:T(8,128)}, u32[]{:S(2)}) copy-start(f32[2,128,8,512]{3,2,1,0:T(8,128)} %param.10) | copy-start | bytes 12582916
  85.5 10.5 %copy-start.5 = (f32[256,1024]{0,1:T(8,128)S(1)}, f32[256,1024]{0,1:T(8,128)}, u32[]{:S(2)}) copy-start(f32[256,1024]{0,1:T(8,128)} %all-gather.3.cloned.1.call-done) | copy-start | bytes 3145732
  85.5 10.5 %copy-start.7 = (f32[256,1024]{1,0:T(8,128)S(1)}, f32[256,1024]{1,0:T(8,128)}, u32[]{:S(2)}) copy-start(f32[256,1024]{1,0:T(8,128)} %param.7) | copy-start | bytes 3145732
  86.6 35.6 %all-gather.5.cloned.1.call-start = ((), (), s32[]{:S(2)}) async-start(), calls=%async_computation.8 | async-start | bytes 1572864 | tf_op jit(solution)/shard_map/all_gather | solution.py:31
  99.1 5.7 %copy-start.2 = (f32[512,512]{1,0:T(8,128)S(1)}, f32[512,512]{1,0:T(8,128)}, u32[]{:S(2)}) copy-start(f32[512,512]{1,0:T(8,128)} %param.13) | copy-start | bytes 3145732
  108.7 82.9 %reduce-scatter.5.cloned.1.call-start = ((), (), s32[]{:S(2)}) async-start(), calls=%async_computation.9 | async-start | bytes 1572864 | tf_op jit(solution)/shard_map/reduce_scatter | solution.py:40
  175.1 2.2 %copy-start.9 = (f32[2,128,8,512]{3,2,1,0:T(8,128)S(1)}, f32[2,128,8,512]{3,2,1,0:T(8,128)}, u32[]{:S(2)}) copy-start(f32[2,128,8,512]{3,2,1,0:T(8,128)} %param.10) | copy-start | bytes 12582916
  181.2 10.5 %copy-start.4 = (f32[256,1024]{1,0:T(8,128)S(1)}, f32[256,1024]{1,0:T(8,128)}, u32[]{:S(2)}) copy-start(f32[256,1024]{1,0:T(8,128)} %all-gather.5.cloned.1.call-done) | copy-start | bytes 3145732
  193.9 7.9 %copy-start.6 = (f32[256,512]{1,0:T(8,128)}, f32[256,512]{1,0:T(8,128)S(1)}, u32[]{:S(2)}) copy-start(f32[256,512]{1,0:T(8,128)S(1)} %fusion.10) | copy-start | bytes 1572868
  194.1 7.8 %copy-start.1 = (f32[256,512]{1,0:T(8,128)S(1)}, f32[256,512]{1,0:T(8,128)}, u32[]{:S(2)}) copy-start(f32[256,512]{1,0:T(8,128)} %convolution_add_fusion.2) | copy-start | bytes 1572868
  194.1 7.8 %copy-start.3 = (f32[512,512]{1,0:T(8,128)S(1)}, f32[512,512]{1,0:T(8,128)}, u32[]{:S(2)}) copy-start(f32[512,512]{1,0:T(8,128)} %param.13) | copy-start | bytes 3145732
Sparse Core Ops, SparseCore 0:
  10.2 15.3 all-gather.2
  86.7 9.2 reduce-scatter.2
  108.8 13.3 all-gather.4
  182.4 9.2 reduce-scatter.4
